TPU v7x, 128 devices: a whole 4x4x4 slice. The times are simulated.
128 devices in a mesh: ctx: 32 (over x, y_lo, z), exp: 4 (over y_hi, core).
Axes of the slice: x: 4, y: 4 (y_hi: 2, y_lo: 2; y = y_hi * 2 + y_lo), z: 4, core: 2. Of those that a mesh axis runs over, the one named last changes fastest.
Arguments:
- residual: bfloat16 [4, 4096, 2048], P('exp', 'ctx'), may hold values from -6 to 6
- query_heads: bfloat16 [4, 4096, 2048], P('exp', 'ctx'), may hold values from -6.5 to 6.5
- key_heads: bfloat16 [4, 4096, 256], P('exp', 'ctx'), may hold values from -6 to 6
- value_heads: bfloat16 [4, 4096, 256], P('exp', 'ctx'), may hold values from -6 to 6
- norm_gain: float32 [2048], replicated, may hold values from 0.1 to 1.9
- chosen_experts: int32 [4, 4096, 8], P('exp', 'ctx'), may hold values from 0 to 127, all different within a row; in each aligned block of 128 rows (0 to 127, 128 to 255, ..., all dimensions but the last counted through in order) at most 9 rows name the same one
- route_weights: float32 [4, 4096, 8], P('exp', 'ctx'), may hold values from 0.05 to 1
- gate_weight: bfloat16 [128, 2048, 768], P(('ctx', 'exp')), may hold values from -0.125 to 0.125
- up_weight: bfloat16 [128, 2048, 768], P(('ctx', 'exp')), may hold values from -0.125 to 0.125
- down_weight: bfloat16 [128, 768, 2048], P(('ctx', 'exp')), may hold values from -0.21875 to 0.21875
- cotangent: bfloat16 [4, 4096, 2048], P('exp', 'ctx'), may hold values from -6 to 6
Outputs:
- layer_out: bfloat16 [4, 4096, 2048], P('exp', 'ctx')
- residual_gradient: bfloat16 [4, 4096, 2048], P('exp', 'ctx')
- query_gradient: bfloat16 [4, 4096, 2048], P('exp', 'ctx')
- key_gradient: bfloat16 [4, 4096, 256], P('exp', 'ctx')
- value_gradient: bfloat16 [4, 4096, 256], P('exp', 'ctx')
- route_gradient: float32 [4, 4096, 8], P('exp', 'ctx')
Inputs may be any that keep to these rules, and one draw needn't show every extreme that they name: `chosen_experts`: among the rows of one device no expert is named by more than 9 rows, a bound that some block reaches; the 8 experts of a row differ.
All inputs are finite; a program needn't handle non-finite values.
Results may differ from a plain program's by a relative error of at most 0.025.
Values may be sent and summed in bfloat16 or wider, within the bound.
A program may use at most 192 MiB of HBM per device.

v0:
```python
import jax
import jax.numpy as jnp
from jax import lax
from jax.sharding import PartitionSpec as P

H = 16
KVH = 2
DH = 128
TOPK = 8
NEG = -1e30
EPSILON = 1e-06


def place_rows(begin_row, row_count):
    row_index = begin_row + jnp.arange(row_count, dtype=jnp.int32)
    return row_index


def over_keys(key_local, value_local, visit, start_state):
    return visit(
        start_state,
        (
            lax.all_gather(key_local, "ctx", axis=0, tiled=True),
            lax.all_gather(value_local, "ctx", axis=0, tiled=True),
        ),
        jnp.int32(0),
    )


def to_experts(rows_out):
    return lax.all_to_all(rows_out, ("ctx", "exp"), split_axis=0, concat_axis=0, tiled=True)


def from_experts(rows_back):
    return lax.all_to_all(rows_back, ("ctx", "exp"), split_axis=0, concat_axis=0, tiled=True)


def forward_tile(state, query_half, query_place, key_block, value_block, key_place, score_scale):
    run_max, run_sum, run_acc = state
    scores = (
        jnp.einsum("ikgd,jkd->kgij", query_half, key_block, preferred_element_type=jnp.float32)
        * score_scale
    )
    allowed = key_place[None, :] <= query_place[:, None]
    scores = jnp.where(allowed, scores, NEG)
    new_max = jnp.maximum(run_max, jnp.max(scores, axis=-1))
    weights = jnp.where(allowed, jnp.exp(scores - new_max[..., None]), 0.0)
    run_sum = jnp.sum(weights, axis=-1)
    run_acc = jnp.einsum(
        "kgij,jkd->kgid",
        weights.astype(jnp.bfloat16),
        value_block,
        preferred_element_type=jnp.float32,
    )
    return (new_max, run_sum, run_acc)


def backward_tile(
    query_acc,
    query_half,
    query_place,
    grad_half,
    log_half,
    dot_half,
    key_block,
    value_block,
    key_place,
    score_scale,
):
    scores = (
        jnp.einsum("ikgd,jkd->kgij", query_half, key_block, preferred_element_type=jnp.float32)
        * score_scale
    )
    allowed = key_place[None, :] <= query_place[:, None]
    weights = jnp.where(allowed, jnp.exp(scores - log_half[..., None]), 0.0)
    value_part = jnp.einsum(
        "kgij,ikgd->jkd",
        weights.astype(jnp.bfloat16),
        grad_half,
        preferred_element_type=jnp.float32,
    )
    grad_weights = jnp.einsum(
        "ikgd,jkd->kgij", grad_half, value_block, preferred_element_type=jnp.float32
    )
    grad_scores = (weights * (grad_weights - dot_half[..., None])).astype(jnp.bfloat16)
    query_acc = (
        jnp.einsum("kgij,jkd->kgid", grad_scores, key_block, preferred_element_type=jnp.float32)
        * score_scale
    )
    key_part = (
        jnp.einsum("kgij,ikgd->jkd", grad_scores, query_half, preferred_element_type=jnp.float32)
        * score_scale
    )
    return (query_acc, key_part, value_part)


def per_device(
    residual,
    query_heads,
    key_heads,
    value_heads,
    norm_gain,
    chosen_experts,
    route_weights,
    gate_weight,
    up_weight,
    down_weight,
    cotangent,
):
    shard_rows = residual.shape[1]
    width = residual.shape[2]
    kv_width = key_heads.shape[2]
    query_width = query_heads.shape[2]
    group_size = H // KVH
    half_rows = shard_rows // 2
    ctx_count = lax.axis_size("ctx")
    seq_rows = shard_rows * ctx_count
    score_scale = DH ** (-0.5)
    ctx_index = lax.axis_index("ctx")
    packed = jnp.concatenate([query_heads[0], key_heads[0], value_heads[0]], axis=1)
    query_local = packed[:, :query_width].reshape(shard_rows, KVH, group_size, DH)
    key_local = packed[:, query_width : query_width + kv_width]
    value_local = packed[:, query_width + kv_width :]
    query_place = place_rows(ctx_index * shard_rows, shard_rows)

    def forward_visit(state, piece, begin_row):
        key_rows, value_rows = piece
        row_count = key_rows.shape[0]
        key_block = key_rows.reshape(row_count, KVH, DH)
        value_block = value_rows.reshape(row_count, KVH, DH)
        key_place = place_rows(begin_row, row_count)
        updated = []
        for which_half in range(2):
            query_half = query_local[which_half * half_rows : (which_half + 1) * half_rows]
            place_half = query_place[which_half * half_rows : (which_half + 1) * half_rows]
            updated.append(
                lax.cond(
                    jnp.min(key_place) <= jnp.max(place_half),
                    lambda inner: forward_tile(
                        inner,
                        query_half,
                        place_half,
                        key_block,
                        value_block,
                        key_place,
                        score_scale,
                    ),
                    lambda inner: inner,
                    state[which_half],
                )
            )
        return tuple(updated)

    start_half = (
        jnp.full((KVH, group_size, half_rows), NEG, jnp.float32),
        jnp.zeros((KVH, group_size, half_rows), jnp.float32),
        jnp.zeros((KVH, group_size, half_rows, DH), jnp.float32),
    )
    halves = over_keys(key_local, value_local, forward_visit, (start_half, start_half))
    attended = jnp.concatenate(
        [acc_half / sum_half[..., None] for max_half, sum_half, acc_half in halves], axis=2
    )
    log_sum = jnp.concatenate(
        [max_half + jnp.log(sum_half) for max_half, sum_half, acc_half in halves], axis=2
    )
    attended_local = (
        jnp.transpose(attended, (2, 0, 1, 3)).reshape(shard_rows, query_width).astype(jnp.bfloat16)
    )
    hidden = (residual[0].astype(jnp.float32) + attended_local.astype(jnp.float32)).astype(
        jnp.bfloat16
    )
    hidden_float = hidden.astype(jnp.float32)
    inverse = lax.rsqrt(jnp.mean(hidden_float * hidden_float, axis=-1, keepdims=True) + EPSILON)
    normed = (hidden_float * inverse * norm_gain).astype(jnp.bfloat16)
    expert_count = ctx_count * lax.axis_size("exp")
    capacity = (9 * shard_rows * TOPK + 8 * expert_count - 1) // (8 * expert_count)
    chosen_flat = chosen_experts[0].reshape(-1)
    onehot_hits = (
        chosen_flat[:, None] == jnp.arange(expert_count, dtype=jnp.int32)[None, :]
    ).astype(jnp.int32)
    earlier = jnp.cumsum(onehot_hits, axis=0) - onehot_hits
    slot_index = jnp.sum(earlier * onehot_hits, axis=1)
    target = chosen_flat * capacity + slot_index
    share_raw = route_weights[0]
    route_total = jnp.sum(share_raw, axis=-1, keepdims=True)
    route_share = share_raw / route_total
    cot_float = cotangent[0].astype(jnp.float32)

    def spread(row_values):
        filled = (
            jnp.zeros((expert_count * capacity, width), jnp.bfloat16).at[target].set(row_values)
        )
        return filled.reshape(expert_count, capacity, width)

    gate_mat = gate_weight[0]
    up_mat = up_weight[0]
    down_mat = down_weight[0]
    incoming = to_experts(spread(jnp.repeat(normed, TOPK, axis=0))).reshape(-1, width)
    gate_act = jnp.dot(incoming, gate_mat, preferred_element_type=jnp.float32)
    up_act = jnp.dot(incoming, up_mat, preferred_element_type=jnp.float32)
    activation = (jax.nn.silu(gate_act) * up_act).astype(jnp.bfloat16)
    produced = jnp.dot(activation, down_mat, preferred_element_type=jnp.float32).astype(
        jnp.bfloat16
    )
    returned = from_experts(produced.reshape(expert_count, capacity, width)).reshape(-1, width)
    picked = returned[target].reshape(shard_rows, TOPK, width)
    moe_sum = jnp.sum(route_share[:, :, None] * picked.astype(jnp.float32), axis=1)
    layer_out = (hidden_float + moe_sum).astype(jnp.bfloat16)
    route_dot = jnp.sum(picked.astype(jnp.float32) * cot_float[:, None, :], axis=-1)
    route_gradient = (
        route_dot - jnp.sum(route_share * route_dot, axis=-1, keepdims=True)
    ) / route_total
    out_cot = (
        (route_share[:, :, None] * cot_float[:, None, :]).astype(jnp.bfloat16).reshape(-1, width)
    )
    cot_in = to_experts(spread(out_cot)).reshape(-1, width)
    act_cot = lax.dot_general(
        cot_in, down_mat, (((1,), (1,)), ((), ())), preferred_element_type=jnp.float32
    )
    sigma_gate = jax.nn.sigmoid(gate_act)
    gate_cot = (act_cot * up_act * sigma_gate * (1.0 + gate_act * (1.0 - sigma_gate))).astype(
        jnp.bfloat16
    )
    up_cot = (act_cot * gate_act * sigma_gate).astype(jnp.bfloat16)
    row_cot = (
        lax.dot_general(
            gate_cot, gate_mat, (((1,), (1,)), ((), ())), preferred_element_type=jnp.float32
        )
        + lax.dot_general(
            up_cot, up_mat, (((1,), (1,)), ((), ())), preferred_element_type=jnp.float32
        )
    ).astype(jnp.bfloat16)
    cot_back = from_experts(row_cot.reshape(expert_count, capacity, width)).reshape(-1, width)
    normed_cot = jnp.sum(
        cot_back[target].reshape(shard_rows, TOPK, width).astype(jnp.float32), axis=1
    )
    gained = norm_gain * normed_cot
    hidden_cot = inverse * gained - hidden_float * inverse**3 * jnp.mean(
        hidden_float * gained, axis=-1, keepdims=True
    )
    residual_gradient = (cot_float + hidden_cot).astype(jnp.bfloat16)
    grad_local = residual_gradient.reshape(shard_rows, KVH, group_size, DH)
    attended_rows = attended_local.reshape(shard_rows, KVH, group_size, DH)
    row_dot = jnp.einsum(
        "ikgd,ikgd->kgi", grad_local, attended_rows, preferred_element_type=jnp.float32
    )

    def backward_visit(state, piece, begin_row):
        query_accs, key_total, value_total = state
        key_rows, value_rows = piece
        row_count = key_rows.shape[0]
        key_block = key_rows.reshape(row_count, KVH, DH)
        value_block = value_rows.reshape(row_count, KVH, DH)
        key_place = place_rows(begin_row, row_count)
        empty_block = jnp.zeros((row_count, KVH, DH), jnp.float32)
        key_sum = empty_block
        value_sum = empty_block
        new_accs = []
        for which_half in range(2):
            lower = which_half * half_rows
            upper = lower + half_rows
            query_half = query_local[lower:upper]
            place_half = query_place[lower:upper]
            grad_half = grad_local[lower:upper]
            log_half = log_sum[:, :, lower:upper]
            dot_half = row_dot[:, :, lower:upper]
            query_acc, key_part, value_part = lax.cond(
                jnp.min(key_place) <= jnp.max(place_half),
                lambda inner: backward_tile(
                    inner,
                    query_half,
                    place_half,
                    grad_half,
                    log_half,
                    dot_half,
                    key_block,
                    value_block,
                    key_place,
                    score_scale,
                ),
                lambda inner: (inner, empty_block, empty_block),
                query_accs[which_half],
            )
            new_accs.append(query_acc)
            key_sum = key_sum + key_part
            value_sum = value_sum + value_part
        key_total = key_sum.reshape(row_count, -1)
        value_total = value_sum.reshape(row_count, -1)
        return (tuple(new_accs), key_total, value_total)

    empty_query = jnp.zeros((KVH, group_size, half_rows, DH), jnp.float32)
    empty_keys = jnp.zeros((seq_rows, kv_width), jnp.float32)
    query_accs, key_total, value_total = over_keys(
        key_local, value_local, backward_visit, ((empty_query, empty_query), empty_keys, empty_keys)
    )
    key_own, value_own = (
        lax.psum_scatter(
            key_total.astype(jnp.bfloat16), "ctx", scatter_dimension=0, tiled=True
        ).astype(jnp.float32),
        lax.psum_scatter(
            value_total.astype(jnp.bfloat16), "ctx", scatter_dimension=0, tiled=True
        ).astype(jnp.float32),
    )
    query_grad = jnp.transpose(jnp.concatenate(query_accs, axis=2), (2, 0, 1, 3)).reshape(
        shard_rows, query_width
    )
    grads_packed = jnp.concatenate(
        [
            query_grad.astype(jnp.bfloat16),
            key_own.astype(jnp.bfloat16),
            value_own.astype(jnp.bfloat16),
        ],
        axis=1,
    )
    query_gradient = grads_packed[:, :query_width]
    key_gradient = grads_packed[:, query_width : query_width + kv_width]
    value_gradient = grads_packed[:, query_width + kv_width :]
    return (
        layer_out[None],
        residual_gradient[None],
        query_gradient[None],
        key_gradient[None],
        value_gradient[None],
        route_gradient[None],
    )


def solution(mesh):
    in_specs = (
        P("exp", "ctx", None),
        P("exp", "ctx", None),
        P("exp", "ctx", None),
        P("exp", "ctx", None),
        P(),
        P("exp", "ctx", None),
        P("exp", "ctx", None),
        P(("ctx", "exp"), None, None),
        P(("ctx", "exp"), None, None),
        P(("ctx", "exp"), None, None),
        P("exp", "ctx", None),
    )
    out_specs = (
        P("exp", "ctx", None),
        P("exp", "ctx", None),
        P("exp", "ctx", None),
        P("exp", "ctx", None),
        P("exp", "ctx", None),
        P("exp", "ctx", None),
    )
    return jax.shard_map(
        per_device, mesh=mesh, in_specs=in_specs, out_specs=out_specs, check_vma=False
    )
```

profile of v0, /device:TPU:0, one launch (start us, length us, event | category | flops | bytes accessed | tf_op | source)
XLA Modules:
  0.0 1245.4 jit_solution(13929531508248828289)
XLA Ops:
  7.2 1.7 copy.64
  9.0 1.6 copy.65
  17.2 2.6 convert_bitcast_fusion
  19.8 10.2 scatter_custom_fusion.1
  29.9 8.1 reshape.375
  38.1 11.7 all-to-all-start.2
  53.6 173.6 %all-gather.5.cloned.1.call-done = bf16[1,4096,256]{1,2,0:T(8,128)(2,1)} async-done(((bf16[1,128,256]{1,2,0:T(8,128)(2,1)}), bf16[1,4096,256]{1,2,0:T(8,128)(2,1)}) %all-gather.5.cloned.1.call-update) | async-done | bytes 2097168 | tf_op jit(solution)/shard_map/all_gather | solution.py:23
  227.2 126.3 %all-gather.7.cloned.1.call-done = bf16[1,4096,256]{1,2,0:T(8,128)(2,1)} async-done(((bf16[1,128,256]{1,2,0:T(8,128)(2,1)}), bf16[1,4096,256]{1,2,0:T(8,128)(2,1)}) %all-gather.7.cloned.1.call-update) | async-done | bytes 2097168 | tf_op jit(solution)/shard_map/all_gather | solution.py:24
  353.5 28.2 %conditional.5 = (f32[2,8,64]{2,1,0:T(8,128)}, f32[2,8,64]{2,1,0:T(8,128)}, f32[2,8,64,128]{3,2,1,0:T(8,128)S(1)}, f32[2,8,64]{2,1,0:T(8,128)S(1)}) conditional(s32[]{:T(128)} %convert_element_type.216, () %tuple.46, (s32[4096]{0:T(1024)S(1)}, s32[64]{0:T(128)S(1)}, bf16[4096,2,128]{0,2,1:T(8,128)(2,1)}, bf16[64,2,8,128]{3,2,1,0:T(8,128)(2,1)S(1)}, ...), branch_computations={%region_6.7_spmd, %region_7.10_spmd} | conditional | flops 2202270720 | bytes 56410400 | solution.py:137
  353.9 9.0 fusion.13
  363.5 8.2 fusion.16
  371.8 9.2 fusion.15
  382.5 29.6 %conditional.4 = (f32[2,8,64]{2,1,0:T(8,128)}, f32[2,8,64]{2,1,0:T(8,128)}, f32[2,8,64,128]{3,2,1,0:T(8,128)S(1)}, f32[2,8,64]{2,1,0:T(8,128)S(1)}) conditional(s32[]{:T(128)} %convert_element_type.215, () %tuple.44, (s32[4096]{0:T(1024)S(1)}, s32[64]{0:T(128)S(1)}, bf16[4096,2,128]{0,2,1:T(8,128)(2,1)}, bf16[64,2,8,128]{3,2,1,0:T(8,128)(2,1)}, ...), branch_computations={%region_1.0_spmd, %region_2.5_spmd} | conditional | flops 2202270720 | bytes 56410400 | solution.py:137
  382.7 10.2 fusion
  393.5 8.2 fusion.3
  401.8 9.2 fusion.2
  412.1 1.5 broadcast_divide_fusion
  417.7 9.9 scatter_custom_fusion
  427.6 8.1 reshape.371
  435.7 8.8 all-to-all-start
  444.5 8.4 reshape.376
  453.0 8.9 fusion.95
  461.9 90.1 %all-to-all-done = bf16[128,9,2048]{2,1,0:T(8,128)(2,1)} async-done(((bf16[128,9,2048]{2,1,0:T(8,128)(2,1)}), bf16[128,9,2048]{2,1,0:T(8,128)(2,1)}, u32[]{:S(2)}, u32[]{:S(2)}) %all-to-all-start) | async-done | bytes 4718624 | tf_op jit(solution)/shard_map/all_to_all | solution.py:31
  552.0 8.5 reshape.372
  560.5 5.9 fusion.103
  566.4 3.9 fusion.99
  570.3 1.7 copy-done.38
  572.1 8.3 fusion.101
  580.3 8.3 add_convert_fusion
  588.6 8.1 reshape.377
  596.7 11.1 all-to-all-start.3
  608.0 1.2 copy.138
  609.2 1.2 copy.136
  610.4 106.7 %all-to-all-done.3 = bf16[128,9,2048]{2,1,0:T(8,128)(2,1)} async-done(((bf16[128,9,2048]{2,1,0:T(8,128)(2,1)}), bf16[128,9,2048]{2,1,0:T(8,128)(2,1)}, u32[]{:S(2)}, u32[]{:S(2)}) %all-to-all-start.3) | async-done | bytes 4718624 | tf_op jit(solution)/shard_map/all_to_all | solution.py:35
  717.1 8.4 reshape.378
  725.5 11.8 gather_fusion.1
  737.3 5.2 convert_reduce_fusion
  743.6 1.2 fusion.128
  744.8 39.8 %conditional.6 = (f32[4096,2,128]{2,0,1:T(8,128)}, f32[4096,2,128]{2,0,1:T(8,128)}, bf16[2,8,64,128]{3,2,1,0:T(8,128)(2,1)S(1)}) conditional(s32[]{:T(128)} %convert_element_type.215, () %tuple.48, (s32[4096]{0:T(1024)S(1)}, s32[64]{0:T(128)S(1)}, bf16[4096,2,128]{0,2,1:T(8,128)(2,1)S(1)}, bf16[64,2,8,128]{3,2,1,0:T(8,128)(2,1)S(1)}, ...), branch_computations={%region_20.21_spmd, %region_21.22_spmd} | conditional | flops 5412226048 | bytes 95461712 | solution.py:267
  746.3 8.1 fusion.42
  754.4 12.9 %fusion.34 = f32[4096,2,128]{2,0,1:T(8,128)} fusion(f32[2,4096,64,8]{1,2,3,0:T(8,128)} %fusion.42, f32[2,8,64]{2,1,0:T(8,128)S(1)} %add.75, pred[64,4096]{1,0:T(8,128)(4,1)S(1)} %broadcast_compare_fusion.2, bf16[64,2,8,128]{3,2,1,0:T(8,128)(2,1)S(1)} %bitcast.303), kind=kOutput, calls=%fused_computation.45 | convolution fusion | flops 1090519040 | bytes 21499904 | tf_op jit(solution)/shard_map/cond/branch_1_fun/kgij,ikgd->jkd/dot_general | solution.py:76
  767.3 9.5 fusion.27
  776.8 2.3 fusion.47
  779.1 5.3 fusion.38
  785.4 40.5 %conditional.7 = (f32[4096,2,128]{2,0,1:T(8,128)}, f32[4096,2,128]{2,0,1:T(8,128)}, bf16[2,8,64,128]{3,2,1,0:T(8,128)(2,1)S(1)}) conditional(s32[]{:T(128)} %convert_element_type.216, () %tuple.50, (s32[4096]{0:T(1024)S(1)}, s32[64]{0:T(128)S(1)}, bf16[4096,2,128]{0,2,1:T(8,128)(2,1)S(1)}, bf16[64,2,8,128]{3,2,1,0:T(8,128)(2,1)S(1)}, ...), branch_computations={%region_22.23_spmd, %region_23.24_spmd} | conditional | flops 5412226048 | bytes 93372696 | solution.py:267
  787.4 8.1 fusion.72
  795.4 12.9 %fusion.64 = f32[4096,2,128]{2,0,1:T(8,128)} fusion(f32[2,4096,64,8]{1,2,3,0:T(8,128)} %fusion.72, f32[2,8,64]{2,1,0:T(8,128)S(1)} %add.76, pred[64,4096]{1,0:T(8,128)(4,1)S(1)} %broadcast_compare_fusion.3, bf16[64,2,8,128]{3,2,1,0:T(8,128)(2,1)S(1)} %bitcast.301), kind=kOutput, calls=%fused_computation.73 | convolution fusion | flops 1090519040 | bytes 21499904 | tf_op jit(solution)/shard_map/cond/branch_1_fun/kgij,ikgd->jkd/dot_general | solution.py:76
  808.3 9.6 fusion.57
  817.9 2.3 fusion.77
  820.2 5.3 fusion.68
  825.9 5.3 copy_bitcast_fusion.1
  831.2 10.0 convolution_convert_fusion
  841.2 8.1 reshape.373
  849.4 10.3 all-to-all-start.1
  859.7 5.3 copy_bitcast_fusion
  865.2 1.1 reshape.379
  866.3 100.4 %all-to-all-done.1 = bf16[128,9,2048]{2,1,0:T(8,128)(2,1)} async-done(((bf16[128,9,2048]{2,1,0:T(8,128)(2,1)}), bf16[128,9,2048]{2,1,0:T(8,128)(2,1)}, u32[]{:S(2)}, u32[]{:S(2)}) %all-to-all-start.1) | async-done | bytes 4718624 | tf_op jit(solution)/shard_map/all_to_all | solution.py:35
  966.8 8.4 reshape.374
  975.2 11.8 gather_fusion
  987.0 6.1 fusion.87
  996.2 2.1 convert_element_type.257
  998.2 3.6 fusion.119
  1001.8 73.6 %reduce-scatter.3.cloned.1.call-done = bf16[128,256]{1,0:T(8,128)(2,1)} async-done(((bf16[4096,256]{1,0:T(8,128)(2,1)}), bf16[128,256]{1,0:T(8,128)(2,1)}) %reduce-scatter.3.cloned.1.call-update) | async-done | bytes 65552 | tf_op jit(solution)/shard_map/reduce_scatter | solution.py:297
  1075.4 162.9 %reduce-scatter.5.cloned.1.call-done = bf16[128,256]{1,0:T(8,128)(2,1)} async-done(((bf16[4096,256]{1,0:T(8,128)(2,1)}), bf16[128,256]{1,0:T(8,128)(2,1)}) %reduce-scatter.5.cloned.1.call-update) | async-done | bytes 65552 | tf_op jit(solution)/shard_map/reduce_scatter | solution.py:300
  (148 shorter events, 25.2 us)
Async XLA Ops:
  7.2 553.3 %copy-start = (bf16[1,2048,768]{2,1,0:T(8,128)(2,1)S(1)}, bf16[1,2048,768]{2,1,0:T(8,128)(2,1)}, u32[]{:S(2)}) copy-start(bf16[1,2048,768]{2,1,0:T(8,128)(2,1)} %param.26) | copy-start | bytes 9437188
  7.2 220.0 %all-gather.5.cloned.1.call-start = ((), (), s32[]{:S(2)}) async-start(), calls=%async_computation.8 | async-start | bytes 2162688 | tf_op jit(solution)/shard_map/all_gather | solution.py:23
  9.0 344.5 %all-gather.7.cloned.1.call-start = ((), (), s32[]{:S(2)}) async-start(), calls=%async_computation.9 | async-start | bytes 2162688 | tf_op jit(solution)/shard_map/all_gather | solution.py:24
  13.1 16.9 %copy-start.25 = (f32[1,128,8]{2,1,0:T(8,128)}, f32[1,128,8]{2,1,0:T(8,128)S(1)}, u32[]{:S(2)}) copy-start(f32[1,128,8]{2,1,0:T(8,128)S(1)} %copy.73) | copy-start | bytes 12292
  13.8 0.6 copy-start.31
  14.8 0.8 copy-start.22
  38.1 397.6 %all-to-all-start.2 = ((bf16[128,9,2048]{2,1,0:T(8,128)(2,1)}), bf16[128,9,2048]{2,1,0:T(8,128)(2,1)}, u32[]{:S(2)}, u32[]{:S(2)}) async-start(bf16[128,9,2048]{2,1,0:T(8,128)(2,1)} %reshape.375), calls=%async_computation.2 | async-start | bytes 16777216 | tf_op jit(solution)/shard_map/all_to_all | solution.py:31
  381.7 0.8 copy-start.23
  412.1 3.3 copy-start.9
  412.1 4.6 copy-start.30
  413.6 0.7 copy-start.18
  413.6 0.8 copy-start.20
  414.4 1.0 copy-start.4
  415.9 0.8 copy-start.6
  416.0 327.6 %copy-start.33 = (f32[128]{0:T(128)}, f32[128]{0:T(128)S(1)}, u32[]{:S(2)}) copy-start(f32[128]{0:T(128)S(1)} %get-tuple-element.208) | copy-start | bytes 1540
  435.7 116.3 %all-to-all-start = ((bf16[128,9,2048]{2,1,0:T(8,128)(2,1)}), bf16[128,9,2048]{2,1,0:T(8,128)(2,1)}, u32[]{:S(2)}, u32[]{:S(2)}) async-start(bf16[128,9,2048]{2,1,0:T(8,128)(2,1)} %reshape.371), calls=%async_computation | async-start | bytes 16777216 | tf_op jit(solution)/shard_map/all_to_all | solution.py:31
  560.5 5.9 copy-start.8
  560.5 5.9 copy-start.35
  566.4 13.9 %copy-start.36 = (f32[1152,768]{1,0:T(8,128)}, f32[1152,768]{1,0:T(8,128)S(1)}, u32[]{:S(2)}) copy-start(f32[1152,768]{1,0:T(8,128)S(1)} %fusion.103) | copy-start | bytes 10616836
  566.4 5.6 copy-start.37
  570.3 1.8 copy-start.38
  596.7 11.2 copy-start.10
  596.7 12.4 copy-start.14
  596.7 120.4 %all-to-all-start.3 = ((bf16[128,9,2048]{2,1,0:T(8,128)(2,1)}), bf16[128,9,2048]{2,1,0:T(8,128)(2,1)}, u32[]{:S(2)}, u32[]{:S(2)}) async-start(bf16[128,9,2048]{2,1,0:T(8,128)(2,1)} %reshape.377), calls=%async_computation.3 | async-start | bytes 16777216 | tf_op jit(solution)/shard_map/all_to_all | solution.py:35
  607.8 467.6 %reduce-scatter.3.cloned.1.call-start = ((), (), s32[]{:S(2)}) async-start(), calls=%async_computation.6 | async-start | bytes 2162688 | tf_op jit(solution)/shard_map/reduce_scatter | solution.py:297
  737.3 5.2 copy-start.7
  737.3 5.7 copy-start.11
  737.3 6.3 copy-start.12
  737.3 6.3 copy-start.13
  737.3 6.3 copy-start.19
  737.3 6.3 copy-start.21
  742.5 2.3 copy-start.3
  742.5 2.3 copy-start.2
  742.5 2.3 copy-start.15
  742.8 2.0 copy-start.34
  743.6 1.3 copy-start.24
  745.3 1.0 copy-start.16
  776.8 2.4 copy-start.17
  784.6 0.7 copy-start.27
  825.9 5.3 copy-start.29
  849.4 117.4 %all-to-all-start.1 = ((bf16[128,9,2048]{2,1,0:T(8,128)(2,1)}), bf16[128,9,2048]{2,1,0:T(8,128)(2,1)}, u32[]{:S(2)}, u32[]{:S(2)}) async-start(bf16[128,9,2048]{2,1,0:T(8,128)(2,1)} %reshape.373), calls=%async_computation.1 | async-start | bytes 16777216 | tf_op jit(solution)/shard_map/all_to_all | solution.py:35
  859.6 378.7 %reduce-scatter.5.cloned.1.call-start = ((), (), s32[]{:S(2)}) async-start(), calls=%async_computation.7 | async-start | bytes 2162688 | tf_op jit(solution)/shard_map/reduce_scatter | solution.py:300
  859.7 5.4 copy-start.26
  859.7 5.4 copy-start.32
  859.7 5.5 copy-start.5
  987.0 7.0 copy-start.28
  987.0 251.3 %copy-start.1 = (bf16[1,2048,768]{2,1,0:T(8,128)(2,1)S(1)}, bf16[1,2048,768]{2,1,0:T(8,128)(2,1)}, u32[]{:S(2)}) copy-start(bf16[1,2048,768]{2,1,0:T(8,128)(2,1)} %param.26) | copy-start | bytes 9437188
Sparse Core Ops, SparseCore 0:
  10.2 217.0 all-gather.4
  229.4 124.1 all-gather.6
  831.3 244.0 reduce-scatter.2
  1078.3 159.9 reduce-scatter.4
where the time goes:
time: 1250 us
  waiting for transfers between devices  834 us (67%)
  matrix products  157 us (13%)
  local copies, waits for them, and re-layouts  124 us (10%)
  other arithmetic  70.5 us (6%)
  starting transfers between devices  42 us (3%)
  between operations  16.2 us (1%)
    all_to_all x2, waiting for transfers between devices, from_experts(): lax.all_to_all(rows_back, ('ctx', 'exp'), split_axis=0, concat_axis=0, ti...  207 us
    all_gather x1, waiting for transfers between devices, over_keys(): lax.all_gather(key_local, 'ctx', axis=0, tiled=True)  174 us
    reduce_scatter x1, waiting for transfers between devices, per_device(): lax.psum_scatter(value_total.astype(jnp.bfloat16), 'ctx', scatter_dimensi...  163 us
    all_gather x1, waiting for transfers between devices, over_keys(): lax.all_gather(value_local, 'ctx', axis=0, tiled=True)  126 us
    all_to_all x2, waiting for transfers between devices, to_experts(): lax.all_to_all(rows_out, ('ctx', 'exp'), split_axis=0, concat_axis=0, til...  90.1 us
    reduce_scatter x1, waiting for transfers between devices, per_device(): lax.psum_scatter(key_total.astype(jnp.bfloat16), 'ctx', scatter_dimension...  73.6 us
    dot_general x2, matrix products, backward_tile(): jnp.einsum('kgij,ikgd->jkd', weights.astype(jnp.bfloat16), grad_half, pre...  25.8 us
  transfers between devices with their start and end apart: 8, of which 7 were waited for; matrix products, arithmetic and copies ran while one was open for 15% of the time, Pallas kernels for 0%

commit v1 on v0

--- a/solution.py
+++ b/solution.py
@@ -2,6 +2,7 @@
 import jax.numpy as jnp
 from jax import lax
 from jax.sharding import PartitionSpec as P
+from jax.lax import all_to_all, axis_size
 
 H = 16
 KVH = 2
@@ -9,6 +10,15 @@
 TOPK = 8
 NEG = -1e30
 EPSILON = 1e-06
+_spread_boxes = lambda incoming_x, peer_axis: jnp.concatenate(
+    all_to_all(
+        jnp.stack([incoming_x for _ in range(axis_size(peer_axis))], axis=0),
+        axis_name=peer_axis,
+        split_axis=0,
+        concat_axis=0,
+    ),
+    axis=0,
+)
 
 
 def place_rows(begin_row, row_count):
@@ -19,10 +29,7 @@
 def over_keys(key_local, value_local, visit, start_state):
     return visit(
         start_state,
-        (
-            lax.all_gather(key_local, "ctx", axis=0, tiled=True),
-            lax.all_gather(value_local, "ctx", axis=0, tiled=True),
-        ),
+        (lax.all_gather(key_local, "ctx", axis=0, tiled=True), _spread_boxes(value_local, "ctx")),
         jnp.int32(0),
     )
 

time: 1250 us -> 1150 us (0.920)
  waiting for transfers between devices: 834 us -> 716 us
    all_gather x1 -> x0, waiting for transfers between devices: 126 us -> none  [over_keys(): lax.all_gather(value_local, 'ctx', axis=0, tiled=True)]
  transfers between devices with their start and end apart: 8 -> 8, of which waited for: 7 -> 7; matrix products, arithmetic and copies ran while one was open for 15% -> 17% of each run, Pallas kernels for 0% -> 0%
where the time goes in v1:
time: 1150 us; the launch traced here: 1140 us
  waiting for transfers between devices  716 us (62%)
  matrix products  157 us (14%)
  local copies, waits for them, and re-layouts  131 us (11%)
  other arithmetic  69.1 us (6%)
  starting transfers between devices  49.2 us (4%)
  between operations  16.2 us (1%)
    all_to_all x2, waiting for transfers between devices, from_experts(): lax.all_to_all(rows_back, ('ctx', 'exp'), split_axis=0, concat_axis=0, ti...  208 us
    all_gather x1, waiting for transfers between devices, over_keys(): lax.all_gather(key_local, 'ctx', axis=0, tiled=True)  175 us
    reduce_scatter x1, waiting for transfers between devices, per_device(): lax.psum_scatter(value_total.astype(jnp.bfloat16), 'ctx', scatter_dimensi...  166 us
    all_to_all x2, waiting for transfers between devices, to_experts(): lax.all_to_all(rows_out, ('ctx', 'exp'), split_axis=0, concat_axis=0, til...  90 us
    reduce_scatter x1, waiting for transfers between devices, per_device(): lax.psum_scatter(key_total.astype(jnp.bfloat16), 'ctx', scatter_dimension...  74.3 us
    dot_general x2, matrix products, backward_tile(): jnp.einsum('kgij,ikgd->jkd', weights.astype(jnp.bfloat16), grad_half, pre...  25.8 us
  transfers between devices with their start and end apart: 8, of which 7 were waited for; matrix products, arithmetic and copies ran while one was open for 17% of the time, Pallas kernels for 0%

profile of v1, /device:TPU:0, one launch (start us, length us, event | category | flops | bytes accessed | tf_op | source)
XLA Modules:
  0.0 1140.9 jit_solution(18320557088927829104)
XLA Ops:
  8.3 1.9 stack.4
  10.2 9.4 all-to-all-start
  24.2 2.6 convert_bitcast_fusion
  26.8 10.1 scatter_custom_fusion.1
  36.9 8.1 reshape.371
  45.1 3.0 all-to-all-done
  48.0 10.5 all-to-all-start.3
  62.4 4.3 copy.66
  66.7 4.2 reshape_reshape.4
  70.8 175.3 %all-gather.3.cloned.1.call-done = bf16[1,4096,256]{1,2,0:T(8,128)(2,1)} async-done(((bf16[1,128,256]{1,2,0:T(8,128)(2,1)}), bf16[1,4096,256]{1,2,0:T(8,128)(2,1)}) %all-gather.3.cloned.1.call-update) | async-done | bytes 2097168 | tf_op jit(solution)/shard_map/all_gather | solution.py:32
  246.2 29.4 %conditional.4 = (f32[2,8,64]{2,1,0:T(8,128)}, f32[2,8,64]{2,1,0:T(8,128)}, f32[2,8,64,128]{3,2,1,0:T(8,128)S(1)}, f32[2,8,64]{2,1,0:T(8,128)S(1)}) conditional(s32[]{:T(128)} %convert_element_type.215, () %tuple.44, (s32[4096]{0:T(1024)S(1)}, s32[64]{0:T(128)S(1)}, bf16[4096,2,128]{0,2,1:T(8,128)(2,1)}, bf16[64,2,8,128]{3,2,1,0:T(8,128)(2,1)}, ...), branch_computations={%region_1.0_spmd, %region_2.5_spmd} | conditional | flops 2202270720 | bytes 56410400 | solution.py:144
  246.6 10.2 fusion
  257.4 8.2 fusion.3
  265.6 9.2 fusion.2
  276.3 28.4 %conditional.5 = (f32[2,8,64]{2,1,0:T(8,128)}, f32[2,8,64]{2,1,0:T(8,128)}, f32[2,8,64,128]{3,2,1,0:T(8,128)S(1)}, f32[2,8,64]{2,1,0:T(8,128)S(1)}) conditional(s32[]{:T(128)} %convert_element_type.216, () %tuple.46, (s32[4096]{0:T(1024)S(1)}, s32[64]{0:T(128)S(1)}, bf16[4096,2,128]{0,2,1:T(8,128)(2,1)}, bf16[64,2,8,128]{3,2,1,0:T(8,128)(2,1)S(1)}, ...), branch_computations={%region_6.7_spmd, %region_7.10_spmd} | conditional | flops 2202270720 | bytes 56410400 | solution.py:144
  276.6 9.0 fusion.13
  286.2 8.2 fusion.16
  294.4 9.2 fusion.15
  304.7 1.4 broadcast_divide_fusion
  310.3 9.9 scatter_custom_fusion
  320.2 8.1 reshape.367
  328.3 7.8 all-to-all-start.1
  336.1 8.4 reshape.372
  344.5 9.0 fusion.95
  353.5 90.0 %all-to-all-done.1 = bf16[128,9,2048]{2,1,0:T(8,128)(2,1)} async-done(((bf16[128,9,2048]{2,1,0:T(8,128)(2,1)}), bf16[128,9,2048]{2,1,0:T(8,128)(2,1)}, u32[]{:S(2)}, u32[]{:S(2)}) %all-to-all-start.1) | async-done | bytes 4718624 | tf_op jit(solution)/shard_map/all_to_all | solution.py:38
  443.5 8.5 reshape.368
  452.0 5.8 fusion.103
  457.9 3.9 fusion.99
  461.8 1.7 copy-done.41
  463.6 8.2 fusion.101
  471.8 8.3 add_convert_fusion
  480.1 8.1 reshape.373
  488.2 11.1 all-to-all-start.4
  499.5 1.2 copy.139
  500.7 1.2 copy.137
  501.9 106.7 %all-to-all-done.4 = bf16[128,9,2048]{2,1,0:T(8,128)(2,1)} async-done(((bf16[128,9,2048]{2,1,0:T(8,128)(2,1)}), bf16[128,9,2048]{2,1,0:T(8,128)(2,1)}, u32[]{:S(2)}, u32[]{:S(2)}) %all-to-all-start.4) | async-done | bytes 4718624 | tf_op jit(solution)/shard_map/all_to_all | solution.py:42
  608.6 8.4 reshape.374
  617.0 11.8 %gather_fusion.1 = bf16[1024,2048]{1,0:T(8,128)(2,1)} fusion(bf16[1152,2048]{1,0:T(8,128)(2,1)} %reshape.374, s32[1024]{0:T(1024)S(1)} %broadcast_clamp_fusion), kind=kCustom, calls=%fused_computation.1 | custom fusion | bytes 8392704 | tf_op jit(solution)/shard_map/gather | solution.py:242
  628.8 5.2 convert_reduce_fusion
  636.3 39.8 %conditional.6 = (f32[4096,2,128]{2,0,1:T(8,128)}, f32[4096,2,128]{2,0,1:T(8,128)}, bf16[2,8,64,128]{3,2,1,0:T(8,128)(2,1)S(1)}) conditional(s32[]{:T(128)} %convert_element_type.215, () %tuple.48, (s32[4096]{0:T(1024)S(1)}, s32[64]{0:T(128)S(1)}, bf16[4096,2,128]{0,2,1:T(8,128)(2,1)S(1)}, bf16[64,2,8,128]{3,2,1,0:T(8,128)(2,1)S(1)}, ...), branch_computations={%region_20.21_spmd, %region_21.22_spmd} | conditional | flops 5412226048 | bytes 95461712 | solution.py:274
  637.8 8.1 fusion.42
  645.8 12.9 %fusion.34 = f32[4096,2,128]{2,0,1:T(8,128)} fusion(f32[2,4096,64,8]{1,2,3,0:T(8,128)} %fusion.42, f32[2,8,64]{2,1,0:T(8,128)S(1)} %add.75, pred[64,4096]{1,0:T(8,128)(4,1)S(1)} %broadcast_compare_fusion.2, bf16[64,2,8,128]{3,2,1,0:T(8,128)(2,1)S(1)} %bitcast.305), kind=kOutput, calls=%fused_computation.45 | convolution fusion | flops 1090519040 | bytes 21499904 | tf_op jit(solution)/shard_map/cond/branch_1_fun/kgij,ikgd->jkd/dot_general | solution.py:83
  658.7 9.5 fusion.27
  668.2 2.3 fusion.47
  670.6 5.3 fusion.38
  676.8 40.5 %conditional.7 = (f32[4096,2,128]{2,0,1:T(8,128)}, f32[4096,2,128]{2,0,1:T(8,128)}, bf16[2,8,64,128]{3,2,1,0:T(8,128)(2,1)S(1)}) conditional(s32[]{:T(128)} %convert_element_type.216, () %tuple.50, (s32[4096]{0:T(1024)S(1)}, s32[64]{0:T(128)S(1)}, bf16[4096,2,128]{0,2,1:T(8,128)(2,1)S(1)}, bf16[64,2,8,128]{3,2,1,0:T(8,128)(2,1)S(1)}, ...), branch_computations={%region_22.23_spmd, %region_23.24_spmd} | conditional | flops 5412226048 | bytes 93372696 | solution.py:274
  678.8 8.1 fusion.72
  686.9 12.9 %fusion.64 = f32[4096,2,128]{2,0,1:T(8,128)} fusion(f32[2,4096,64,8]{1,2,3,0:T(8,128)} %fusion.72, f32[2,8,64]{2,1,0:T(8,128)S(1)} %add.76, pred[64,4096]{1,0:T(8,128)(4,1)S(1)} %broadcast_compare_fusion.3, bf16[64,2,8,128]{3,2,1,0:T(8,128)(2,1)S(1)} %bitcast.303), kind=kOutput, calls=%fused_computation.73 | convolution fusion | flops 1090519040 | bytes 21499904 | tf_op jit(solution)/shard_map/cond/branch_1_fun/kgij,ikgd->jkd/dot_general | solution.py:83
  699.8 9.6 fusion.57
  709.4 2.3 fusion.77
  711.7 5.3 fusion.68
  717.3 5.3 copy_bitcast_fusion.1
  722.7 10.0 convolution_convert_fusion
  732.7 8.1 reshape.369
  740.8 10.3 all-to-all-start.2
  751.1 5.3 copy_bitcast_fusion
  757.8 100.9 %all-to-all-done.2 = bf16[128,9,2048]{2,1,0:T(8,128)(2,1)} async-done(((bf16[128,9,2048]{2,1,0:T(8,128)(2,1)}), bf16[128,9,2048]{2,1,0:T(8,128)(2,1)}, u32[]{:S(2)}, u32[]{:S(2)}) %all-to-all-start.2) | async-done | bytes 4718624 | tf_op jit(solution)/shard_map/all_to_all | solution.py:42
  858.7 8.4 reshape.370
  867.1 11.8 %gather_fusion = bf16[1024,2048]{1,0:T(8,128)(2,1)} fusion(bf16[1152,2048]{1,0:T(8,128)(2,1)} %reshape.370, s32[1024]{0:T(1024)S(1)} %broadcast_clamp_fusion), kind=kCustom, calls=%fused_computation | custom fusion | bytes 8392704 | tf_op jit(solution)/shard_map/gather | solution.py:213
  878.8 6.1 fusion.87
  888.0 2.1 convert_element_type.257
  890.1 3.6 fusion.119
  893.7 74.3 %reduce-scatter.3.cloned.1.call-done = bf16[128,256]{1,0:T(8,128)(2,1)} async-done(((bf16[4096,256]{1,0:T(8,128)(2,1)}), bf16[128,256]{1,0:T(8,128)(2,1)}) %reduce-scatter.3.cloned.1.call-update) | async-done | bytes 65552 | tf_op jit(solution)/shard_map/reduce_scatter | solution.py:304
  968.0 165.9 %reduce-scatter.5.cloned.1.call-done = bf16[128,256]{1,0:T(8,128)(2,1)} async-done(((bf16[4096,256]{1,0:T(8,128)(2,1)}), bf16[128,256]{1,0:T(8,128)(2,1)}) %reduce-scatter.5.cloned.1.call-update) | async-done | bytes 65552 | tf_op jit(solution)/shard_map/reduce_scatter | solution.py:307
  (156 shorter events, 26.5 us)
Async XLA Ops:
  7.2 444.9 %copy-start = (bf16[1,2048,768]{2,1,0:T(8,128)(2,1)S(1)}, bf16[1,2048,768]{2,1,0:T(8,128)(2,1)}, u32[]{:S(2)}) copy-start(bf16[1,2048,768]{2,1,0:T(8,128)(2,1)} %param.26) | copy-start | bytes 9437188
  7.2 12.5 %copy-start.31 = (bf16[1,128,256]{2,1,0:T(8,128)(2,1)S(1)}, bf16[1,128,256]{2,1,0:T(8,128)(2,1)}, u32[]{:S(2)}) copy-start(bf16[1,128,256]{2,1,0:T(8,128)(2,1)} %param.21) | copy-start | bytes 196612
  7.2 13.2 %copy-start.33 = (s32[1,128,8]{1,2,0:T(8,128)S(1)}, s32[1,128,8]{1,2,0:T(8,128)}, u32[]{:S(2)}) copy-start(s32[1,128,8]{1,2,0:T(8,128)} %param.24) | copy-start | bytes 12292
  7.2 13.5 %copy-start.32 = (f32[1,128,8]{1,2,0:T(8,128)S(1)}, f32[1,128,8]{1,2,0:T(8,128)}, u32[]{:S(2)}) copy-start(f32[1,128,8]{1,2,0:T(8,128)} %param.25) | copy-start | bytes 12292
  10.2 37.8 %all-to-all-start = ((bf16[32,128,256]{1,2,0:T(8,128)(2,1)}), bf16[32,128,256]{1,2,0:T(8,128)(2,1)}, u32[]{:S(2)}, u32[]{:S(2)}) async-start(bf16[32,128,256]{1,2,0:T(8,128)(2,1)} %stack.4), calls=%async_computation | async-start | bytes 4194304 | tf_op jit(solution)/shard_map/all_to_all | solution.py:14
  19.6 226.6 %all-gather.3.cloned.1.call-start = ((), (), s32[]{:S(2)}) async-start(), calls=%async_computation.9 | async-start | bytes 2162688 | tf_op jit(solution)/shard_map/all_gather | solution.py:32
  20.8 16.1 %copy-start.25 = (f32[1,128,8]{2,1,0:T(8,128)}, f32[1,128,8]{2,1,0:T(8,128)S(1)}, u32[]{:S(2)}) copy-start(f32[1,128,8]{2,1,0:T(8,128)S(1)} %copy.74) | copy-start | bytes 12292
  20.8 0.5 copy-start.34
  21.7 0.8 copy-start.22
  48.0 280.3 %all-to-all-start.3 = ((bf16[128,9,2048]{2,1,0:T(8,128)(2,1)}), bf16[128,9,2048]{2,1,0:T(8,128)(2,1)}, u32[]{:S(2)}, u32[]{:S(2)}) async-start(bf16[128,9,2048]{2,1,0:T(8,128)(2,1)} %reshape.371), calls=%async_computation.3 | async-start | bytes 16777216 | tf_op jit(solution)/shard_map/all_to_all | solution.py:38
  275.5 0.8 copy-start.23
  304.7 3.3 copy-start.9
  304.7 4.6 copy-start.30
  306.2 0.7 copy-start.18
  306.2 0.8 copy-start.20
  307.0 1.0 copy-start.4
  308.6 0.8 copy-start.6
  308.6 326.5 %copy-start.36 = (f32[128]{0:T(128)}, f32[128]{0:T(128)S(1)}, u32[]{:S(2)}) copy-start(f32[128]{0:T(128)S(1)} %get-tuple-element.208) | copy-start | bytes 1540
  328.3 115.2 %all-to-all-start.1 = ((bf16[128,9,2048]{2,1,0:T(8,128)(2,1)}), bf16[128,9,2048]{2,1,0:T(8,128)(2,1)}, u32[]{:S(2)}, u32[]{:S(2)}) async-start(bf16[128,9,2048]{2,1,0:T(8,128)(2,1)} %reshape.367), calls=%async_computation.1 | async-start | bytes 16777216 | tf_op jit(solution)/shard_map/all_to_all | solution.py:38
  452.0 5.9 copy-start.8
  452.0 5.9 copy-start.38
  457.9 13.9 %copy-start.39 = (f32[1152,768]{1,0:T(8,128)}, f32[1152,768]{1,0:T(8,128)S(1)}, u32[]{:S(2)}) copy-start(f32[1152,768]{1,0:T(8,128)S(1)} %fusion.103) | copy-start | bytes 10616836
  457.9 5.6 copy-start.40
  461.8 1.7 copy-start.41
  488.2 11.2 copy-start.10
  488.2 12.5 %copy-start.14 = (f32[16,8,16,128]{3,1,2,0:T(8,128)S(1)}, f32[16,8,16,128]{3,1,2,0:T(8,128)}, u32[]{:S(2)}) copy-start(f32[16,8,16,128]{3,1,2,0:T(8,128)} %get-tuple-element.204) | copy-start | bytes 3145732
  488.2 120.4 %all-to-all-start.4 = ((bf16[128,9,2048]{2,1,0:T(8,128)(2,1)}), bf16[128,9,2048]{2,1,0:T(8,128)(2,1)}, u32[]{:S(2)}, u32[]{:S(2)}) async-start(bf16[128,9,2048]{2,1,0:T(8,128)(2,1)} %reshape.373), calls=%async_computation.4 | async-start | bytes 16777216 | tf_op jit(solution)/shard_map/all_to_all | solution.py:42
  499.3 468.7 %reduce-scatter.3.cloned.1.call-start = ((), (), s32[]{:S(2)}) async-start(), calls=%async_computation.7 | async-start | bytes 2162688 | tf_op jit(solution)/shard_map/reduce_scatter | solution.py:304
  628.7 5.2 copy-start.7
  628.8 5.7 copy-start.11
  628.8 6.3 copy-start.12
  628.8 6.3 copy-start.13
  628.8 6.3 copy-start.19
  628.8 6.3 copy-start.21
  634.0 2.3 copy-start.3
  634.0 2.3 copy-start.2
  634.0 2.3 copy-start.15
  634.3 2.0 copy-start.37
  635.0 1.3 copy-start.24
  636.7 1.0 copy-start.16
  668.2 2.4 copy-start.17
  676.1 0.7 copy-start.27
  717.3 5.3 copy-start.29
  740.8 117.9 %all-to-all-start.2 = ((bf16[128,9,2048]{2,1,0:T(8,128)(2,1)}), bf16[128,9,2048]{2,1,0:T(8,128)(2,1)}, u32[]{:S(2)}, u32[]{:S(2)}) async-start(bf16[128,9,2048]{2,1,0:T(8,128)(2,1)} %reshape.369), calls=%async_computation.2 | async-start | bytes 16777216 | tf_op jit(solution)/shard_map/all_to_all | solution.py:42
  751.1 382.8 %reduce-scatter.5.cloned.1.call-start = ((), (), s32[]{:S(2)}) async-start(), calls=%async_computation.8 | async-start | bytes 2162688 | tf_op jit(solution)/shard_map/reduce_scatter | solution.py:307
  751.1 5.4 copy-start.26
  751.1 5.4 copy-start.35
  751.1 5.5 copy-start.5
  878.8 7.1 copy-start.28
  878.8 255.1 %copy-start.1 = (bf16[1,2048,768]{2,1,0:T(8,128)(2,1)S(1)}, bf16[1,2048,768]{2,1,0:T(8,128)(2,1)}, u32[]{:S(2)}) copy-start(bf16[1,2048,768]{2,1,0:T(8,128)(2,1)} %param.26) | copy-start | bytes 9437188
Sparse Core Ops, SparseCore 0:
  22.6 223.5 all-gather.2
  722.8 245.1 reduce-scatter.2
  971.1 162.7 reduce-scatter.4
